TPU v7x, 32 devices: a whole 2x2x4 slice. The times are simulated.
32 devices in a mesh: dp: 4 (over y, x), wide: 8 (over z, core).
Axes of the slice: x: 2, y: 2, z: 4, core: 2. Of those that a mesh axis runs over, the one named last changes fastest.
Arguments:
- clips: bfloat16 [4, 8, 4, 128, 512], P('dp', 'wide'), may hold values from -8 to 8
- w_spatial: bfloat16 [4608, 512], P(None, 'dp'), may hold values from -0.09375 to 0.09375
- w_time: bfloat16 [1536, 512], replicated, may hold values from -0.15625 to 0.15625
- norm_gain: float32 [512], replicated, may hold values from 0.1 to 1.9
- norm_bias: float32 [512], replicated, may hold values from -0.6 to 0.6
- grad_out: bfloat16 [4, 8, 512, 512], P('dp', None, 'wide'), may hold values from -6 to 6
Outputs:
- grad_clips: bfloat16 [4, 8, 4, 128, 512], P('dp', 'wide')
- spatial_grad: float32 [4608, 512], P('dp', 'wide')
- time_grad: float32 [1536, 512], P('dp', 'wide')
All inputs are finite; a program needn't handle non-finite values.
Results may differ from a plain program's by a relative error of at most 0.009.
Values may be sent and summed in bfloat16 or wider, within the bound.
No kernel may reach another device: no remote copies, remote signals or barrier semaphores. Data moves between devices by JAX's collectives and lax.ppermute only.
A program may use at most 128 MiB of HBM per device.

v0:
```python
import jax
import jax.numpy as jnp
from jax import lax
from jax.sharding import PartitionSpec as P

G = 32
FRAMES = 8
EPSILON = 1e-06
CONTRACT_ROWS = (((0,), (0,)), ((), ()))
CONTRACT_COLS = (((1,), (1,)), ((), ()))


def pad_frames(frames):
    return jnp.pad(frames, ((0, 0), (1, 1), (1, 1), (0, 0)))


def spatial_forward(frames, weights):
    frame_total, row_count, col_count, chan_count = frames.shape
    padded = pad_frames(frames)
    accum_out = jnp.zeros((frame_total * row_count * col_count, weights.shape[1]), jnp.float32)
    for tap_index in range(9):
        row_off, col_off = (tap_index // 3, tap_index % 3)
        window = padded[:, row_off : row_off + row_count, col_off : col_off + col_count, :].reshape(
            -1, chan_count
        )
        tap_weight = weights[tap_index * chan_count : (tap_index + 1) * chan_count]
        accum_out = accum_out + jnp.dot(window, tap_weight, preferred_element_type=jnp.float32)
    return accum_out.reshape(frame_total, row_count, col_count, -1)


def spatial_backward(frames, grad_hidden, weights):
    frame_total, row_count, col_count, chan_count = frames.shape
    padded_in = pad_frames(frames)
    padded_grad = pad_frames(grad_hidden)
    grad_flat = grad_hidden.reshape(-1, chan_count)
    grad_input = jnp.zeros((frame_total * row_count * col_count, chan_count), jnp.float32)
    tap_grads = []
    for tap_index in range(9):
        row_off, col_off = (tap_index // 3, tap_index % 3)
        window = padded_in[
            :, row_off : row_off + row_count, col_off : col_off + col_count, :
        ].reshape(-1, chan_count)
        tap_grads.append(
            lax.dot_general(window, grad_flat, CONTRACT_ROWS, preferred_element_type=jnp.float32)
        )
        flipped = padded_grad[
            :, 2 - row_off : 2 - row_off + row_count, 2 - col_off : 2 - col_off + col_count, :
        ].reshape(-1, chan_count)
        tap_weight = weights[tap_index * chan_count : (tap_index + 1) * chan_count]
        grad_input = grad_input + lax.dot_general(
            flipped, tap_weight, CONTRACT_COLS, preferred_element_type=jnp.float32
        )
    return (grad_input.reshape(frames.shape), jnp.concatenate(tap_grads, axis=0))


def norm_forward(hidden, norm_gain, norm_bias):
    frame_total, row_count, col_count, chan_count = hidden.shape
    grouped = hidden.astype(jnp.float32).reshape(
        frame_total, row_count * col_count, G, chan_count // G
    )
    group_mean = jnp.mean(grouped, axis=(1, 3), keepdims=True)
    centered = grouped - group_mean
    variance = jnp.mean(centered * centered, axis=(1, 3), keepdims=True)
    inv_std = lax.rsqrt(variance + EPSILON)
    normed = centered * inv_std
    preact = normed.reshape(hidden.shape) * norm_gain + norm_bias
    return (preact, normed, inv_std)


def norm_backward(grad_act, preact, normed, inv_std, norm_gain):
    sigmoid_z = jax.nn.sigmoid(preact)
    grad_pre = grad_act.astype(jnp.float32) * sigmoid_z * (1.0 + preact * (1.0 - sigmoid_z))
    grad_normed = (grad_pre * norm_gain).reshape(normed.shape)
    mean_grad = jnp.mean(grad_normed, axis=(1, 3), keepdims=True)
    mean_proj = jnp.mean(grad_normed * normed, axis=(1, 3), keepdims=True)
    return ((grad_normed - mean_grad - normed * mean_proj) * inv_std).reshape(preact.shape)


def temporal_backward(tiles, grad_out, w_time):
    clip_count, frame_total, pix_count, chan_count = tiles.shape
    grad_act = jnp.zeros(tiles.shape, jnp.float32)
    tap_grads = []
    for tap_index in range(3):
        kept = frame_total - tap_index
        earlier = tiles[:, :kept].reshape(-1, chan_count)
        later = grad_out[:, tap_index:].reshape(-1, chan_count)
        tap_grads.append(
            lax.dot_general(earlier, later, CONTRACT_ROWS, preferred_element_type=jnp.float32)
        )
        tap_weight = w_time[tap_index * chan_count : (tap_index + 1) * chan_count]
        back_part = lax.dot_general(
            later, tap_weight, CONTRACT_COLS, preferred_element_type=jnp.float32
        )
        back_part = back_part.reshape(clip_count, kept, pix_count, chan_count)
        grad_act = grad_act + jnp.pad(back_part, ((0, 0), (0, tap_index), (0, 0), (0, 0)))
    return (jnp.concatenate(tap_grads, axis=0), grad_act)


def shards(clips, w_spatial, w_time, norm_gain, norm_bias, grad_out):
    group_count, frame_count, row_count, col_count, chan_count = clips.shape
    frames = clips.reshape(group_count * frame_count, row_count, col_count, chan_count)
    weights = lax.all_gather(w_spatial, "dp", axis=1, tiled=True)
    hidden = spatial_forward(frames, weights).astype(jnp.bfloat16)
    preact, normed, inv_std = norm_forward(hidden, norm_gain, norm_bias)
    act = (
        jax.nn.silu(preact)
        .astype(jnp.bfloat16)
        .reshape(group_count, frame_count, row_count * col_count, chan_count)
    )
    tiles = lax.all_to_all(act, "wide", split_axis=2, concat_axis=1, tiled=True)
    tile_shape = tiles.shape
    by_clip = tiles.reshape(-1, FRAMES, tile_shape[2], tile_shape[3])
    grad_clipwise = grad_out.reshape(by_clip.shape)
    time_raw, grad_act = temporal_backward(by_clip, grad_clipwise, w_time)
    grad_act = grad_act.astype(jnp.bfloat16).reshape(tile_shape)
    returned = lax.all_to_all(grad_act, "wide", split_axis=1, concat_axis=2, tiled=True)
    grad_hidden = norm_backward(
        returned.reshape(frames.shape), preact, normed, inv_std, norm_gain
    ).astype(jnp.bfloat16)
    grad_input, spatial_raw = spatial_backward(frames, grad_hidden, weights)
    position_total = (
        group_count
        * frame_count
        * row_count
        * col_count
        * lax.axis_size("wide")
        * lax.axis_size("dp")
    )
    grad_scale = float(position_total) ** (-0.5)
    partial_pair = (
        lax.psum_scatter(spatial_raw, "wide", scatter_dimension=1, tiled=True),
        lax.psum_scatter(time_raw, "wide", scatter_dimension=1, tiled=True),
    )
    spatial_sum, time_sum = (
        lax.psum_scatter(partial_pair[0], "dp", scatter_dimension=0, tiled=True),
        lax.psum_scatter(partial_pair[1], "dp", scatter_dimension=0, tiled=True),
    )
    grad_clips = grad_input.astype(jnp.bfloat16).reshape(clips.shape)
    return (grad_clips, spatial_sum * grad_scale, time_sum * grad_scale)


def solution(mesh):
    return jax.shard_map(
        shards,
        mesh=mesh,
        in_specs=(
            P("dp", "wide", None, None, None),
            P(None, "dp"),
            P(),
            P(),
            P(),
            P("dp", None, "wide", None),
        ),
        out_specs=(P("dp", "wide", None, None, None), P("dp", "wide"), P("dp", "wide")),
        check_vma=False,
    )
```

profile of v0, /device:TPU:0, one launch (start us, length us, event | category | flops | bytes accessed | tf_op | source)
XLA Modules:
  0.0 337.8 jit_solution(4861131859740784181)
XLA Ops:
  7.9 1.6 convolution_bitcast_fusion.13
  9.5 1.6 convolution_bitcast_fusion.12
  11.1 2.3 fusion.15
  13.4 6.4 %all-to-all-start = ((bf16[1,8,64,512]{3,2,0,1:T(8,128)(2,1)}), bf16[1,8,64,512]{3,2,0,1:T(8,128)(2,1)S(1)}, u32[]{:S(2)}, u32[]{:S(2)}) async-start(bf16[1,8,64,512]{3,2,0,1:T(8,128)(2,1)} %fusion.15), calls=%async_computation | async-start | bytes 1048576 | tf_op jit(solution)/shard_map/all_to_all | solution.py:116
  20.1 2.5 pad_slice_fusion
  22.6 2.1 copy.46
  24.7 2.0 copy.40
  26.7 2.1 copy.41
  28.8 2.0 copy.42
  30.8 2.0 copy.43
  32.9 2.0 copy.44
  34.9 1.0 copy.45
  36.9 32.4 %all-gather.2.cloned.1.call-done = bf16[4608,512]{1,0:T(8,128)(2,1)} async-done(((bf16[4608,128]{1,0:T(8,128)(2,1)}), bf16[4608,512]{1,0:T(8,128)(2,1)}) %all-gather.2.cloned.1.call-update) | async-done | bytes 4718608 | tf_op jit(solution)/shard_map/all_gather | solution.py:102
  69.4 1.8 fusion.58
  71.2 1.6 convolution_add_fusion.15
  77.0 1.6 fusion.68
  80.1 1.8 copy.58
  82.4 5.6 %reduce.16 = bf16[512,512]{1,0:T(8,128)(2,1)} reduce(bf16[512,1,1,512]{3,2,1,0:T(2,128)(2,1)} %bitcast.222, bf16[]{:T(256)} %broadcast.543), dimensions={1,2}, to_apply=%bitcast.194.reduce_sub_computation | reduce | bytes 1048578
  88.0 2.2 reshape.596
  90.2 20.0 %all_to_all.21 = bf16[8,2,16384]{2,1,0:T(2,128)(2,1)} all-to-all(bf16[8,2,16384]{2,1,0:T(2,128)(2,1)} %reshape.596), channel_id=1, replica_groups=mesh['dp'=4,'wide'=8] {'wide'}, dimensions={0} | all-to-all | bytes 1048576 | tf_op jit(solution)/shard_map/all_to_all | solution.py:110
  110.2 3.5 %reshape.597 = bf16[512,1,1,512]{3,2,1,0:T(2,128)(2,1)} reshape(bf16[8,2,16384]{2,1,0:T(2,128)(2,1)} %all_to_all.21) | data formatting | bytes 1048576
  113.7 1.3 copy.55
  116.4 2.0 pad_maximum_fusion
  118.4 3.6 %copy.53 = f32[1536,512]{0,1:T(8,128)} copy(f32[1536,512]{1,0:T(8,128)} %pad_maximum_fusion) | data formatting | bytes 6291456
  122.0 1.5 multiply_convert_fusion.1
  123.6 1.5 fusion.8
  125.0 1.4 fusion.7
  126.4 1.5 fusion.6
  127.9 1.5 fusion.5
  129.5 1.5 fusion.4
  130.9 1.5 fusion.3
  132.4 1.5 fusion.2
  133.9 1.4 fusion.1
  135.3 1.5 fusion
  136.8 9.7 %copy.51 = f32[4608,512]{0,1:T(8,128)} copy(f32[4608,512]{1,0:T(8,128)} %fusion) | data formatting | bytes 18874368
  146.6 13.9 %reduce-scatter.15.cloned.1.call-done = f32[64,1536]{1,0:T(8,128)} async-done(((f32[512,1536]{1,0:T(8,128)}), f32[64,1536]{1,0:T(8,128)}) %reduce-scatter.15.cloned.1.call-update) | async-done | bytes 393232
  160.5 2.2 copy.54
  163.4 1.9 pad_slice_fusion.8
  165.3 1.5 fusion.56
  166.8 94.7 %reduce-scatter.13.cloned.1.call-done = f32[64,4608]{1,0:T(8,128)} async-done(((f32[512,4608]{1,0:T(8,128)}), f32[64,4608]{1,0:T(8,128)}) %reduce-scatter.13.cloned.1.call-update) | async-done | bytes 1179664
  261.5 2.9 copy.52
  264.5 1.8 convolution_add_fusion.7
  266.3 1.7 convolution_add_fusion.6
  268.1 1.7 convolution_add_fusion.5
  271.8 1.3 fusion.14
  273.1 15.9 %reduce-scatter.11.cloned.1.call-done = f32[384,64]{1,0:T(8,128)} async-done(((f32[1536,64]{1,0:T(8,128)}), f32[384,64]{1,0:T(8,128)}) %reduce-scatter.11.cloned.1.call-update) | async-done | bytes 98320 | tf_op jit(solution)/shard_map/reduce_scatter | solution.py:136
  290.6 38.6 %reduce-scatter.9.cloned.1.call-done = f32[1152,64]{1,0:T(8,128)} async-done(((f32[4608,64]{1,0:T(8,128)}), f32[1152,64]{1,0:T(8,128)}) %reduce-scatter.9.cloned.1.call-update) | async-done | bytes 294928 | tf_op jit(solution)/shard_map/reduce_scatter | solution.py:135
  329.2 1.1 broadcast_multiply_fusion
  (91 shorter events, 14.8 us)
Async XLA Ops:
  7.2 3.9 %copy-start.1 = (bf16[1,8,64,512]{3,2,1,0:T(8,128)(2,1)S(1)}, bf16[1,8,64,512]{3,2,1,0:T(8,128)(2,1)}, u32[]{:S(2)}) copy-start(bf16[1,8,64,512]{3,2,1,0:T(8,128)(2,1)} %param.11) | copy-start | bytes 1572868
  7.2 12.6 %copy-start.2 = (bf16[1,1,4,128,512]{4,3,2,1,0:T(8,128)(2,1)S(1)}, bf16[1,1,4,128,512]{4,3,2,1,0:T(8,128)(2,1)}, u32[]{:S(2)}) copy-start(bf16[1,1,4,128,512]{4,3,2,1,0:T(8,128)(2,1)} %param.6) | copy-start | bytes 1572868
  7.2 62.2 %all-gather.2.cloned.1.call-start = ((), (), s32[]{:S(2)}) async-start(), calls=%async_computation.6 | async-start | bytes 5898240 | tf_op jit(solution)/shard_map/all_gather | solution.py:102
  13.4 63.6 %all-to-all-start = ((bf16[1,8,64,512]{3,2,0,1:T(8,128)(2,1)}), bf16[1,8,64,512]{3,2,0,1:T(8,128)(2,1)S(1)}, u32[]{:S(2)}, u32[]{:S(2)}) async-start(bf16[1,8,64,512]{3,2,0,1:T(8,128)(2,1)} %fusion.15), calls=%async_computation | async-start | bytes 1048576 | tf_op jit(solution)/shard_map/all_to_all | solution.py:116
  19.8 140.7 %reduce-scatter.15.cloned.1.call-start = ((), (), s32[]{:S(2)}) async-start(), calls=%async_computation.10 | async-start | bytes 3538944
  35.9 37.4 %copy-start.12 = (bf16[1,4,128,512]{3,2,1,0:T(8,128)(2,1)S(1)}, bf16[1,4,128,512]{3,2,1,0:T(8,128)(2,1)}, u32[]{:S(2)}) copy-start(bf16[1,4,128,512]{3,2,1,0:T(8,128)(2,1)} %copy.42) | copy-start | bytes 1572868
  36.9 35.9 %copy-start.13 = (bf16[1,4,128,512]{3,2,1,0:T(8,128)(2,1)S(1)}, bf16[1,4,128,512]{3,2,1,0:T(8,128)(2,1)}, u32[]{:S(2)}) copy-start(bf16[1,4,128,512]{3,2,1,0:T(8,128)(2,1)} %copy.41) | copy-start | bytes 1572868
  69.4 3.4 %copy-start = (bf16[4608,512]{1,0:T(8,128)(2,1)S(1)}, bf16[4608,512]{1,0:T(8,128)(2,1)}, u32[]{:S(2)}) copy-start(bf16[4608,512]{1,0:T(8,128)(2,1)} %all-gather.2.cloned.1.call-done) | copy-start | bytes 14155780
  72.8 1.4 copy-start.11
  73.3 1.4 copy-start.10
  73.7 1.4 copy-start.9
  74.2 1.4 copy-start.8
  74.7 2.3 copy-start.14
  74.7 2.3 copy-start.15
  122.0 139.5 %reduce-scatter.13.cloned.1.call-start = ((), (), s32[]{:S(2)}) async-start(), calls=%async_computation.9 | async-start | bytes 10616832
  123.5 5.9 %copy-start.3 = (bf16[1,1,4,128,512]{4,3,2,1,0:T(8,128)(2,1)S(1)}, bf16[1,1,4,128,512]{4,3,2,1,0:T(8,128)(2,1)}, u32[]{:S(2)}) copy-start(bf16[1,1,4,128,512]{4,3,2,1,0:T(8,128)(2,1)} %param.6) | copy-start | bytes 1572868
  146.5 142.4 %reduce-scatter.11.cloned.1.call-start = ((), (), s32[]{:S(2)}) async-start(), calls=%async_computation.8 | async-start | bytes 983040 | tf_op jit(solution)/shard_map/reduce_scatter | solution.py:136
  162.7 166.6 %reduce-scatter.9.cloned.1.call-start = ((), (), s32[]{:S(2)}) async-start(), calls=%async_computation.7 | async-start | bytes 2949120 | tf_op jit(solution)/shard_map/reduce_scatter | solution.py:135
  261.5 8.3 %slice-start = ((s8[4718592]{0:T(1024)(128)(4,1)}), s8[524288]{0:T(1024)(128)(4,1)S(1)}, s32[]{:S(2)}) async-start(s8[4718592]{0:T(1024)(128)(4,1)} %bitcast.214), calls=%async_computation.11 | async-start | bytes 1048576
  264.5 5.3 %slice-start.1 = ((s8[4718592]{0:T(1024)(128)(4,1)}), s8[4194304]{0:T(1024)(128)(4,1)S(1)}, s32[]{:S(2)}) async-start(s8[4718592]{0:T(1024)(128)(4,1)} %bitcast.214), calls=%async_computation.12 | async-start | bytes 8388608
  266.3 4.0 %copy-start.7 = (bf16[1,4,128,512]{3,2,1,0:T(8,128)(2,1)S(1)}, bf16[1,4,128,512]{3,2,1,0:T(8,128)(2,1)}, u32[]{:S(2)}) copy-start(bf16[1,4,128,512]{3,2,1,0:T(8,128)(2,1)} %get-tuple-element.24) | copy-start | bytes 1572868
  268.0 2.8 copy-start.6
  269.8 1.5 copy-start.5
  270.3 1.5 copy-start.4
Sparse Core Ops, SparseCore 0:
  9.8 59.5 all-gather.1
  122.1 38.3 reduce-scatter.14
  162.8 98.6 reduce-scatter.12
  264.3 24.6 reduce-scatter.10
  291.8 37.3 reduce-scatter.8
where the time goes:
time: 339 us; the launch traced here: 338 us
  waiting for transfers between devices  196 us (58%)
  local copies, waits for them, and re-layouts  49.4 us (15%)
  matrix products  36.5 us (11%)
  blocking collectives  20 us (6%)
  other arithmetic  14.8 us (4%)
  between operations  14.3 us (4%)
  starting transfers between devices  6.55 us (2%)
    unnamed x7, waiting for transfers between devices  109 us
    reduce_scatter x1, waiting for transfers between devices, shards(): lax.psum_scatter(partial_pair[0], 'dp', scatter_dimension=0, tiled=True)  38.6 us
    all_gather x1, waiting for transfers between devices, shards(): weights = lax.all_gather(w_spatial, 'dp', axis=1, tiled=True)  32.4 us
    unnamed x47, local copies, waits for them, and re-layouts  27.9 us
    all_to_all x1, blocking collectives, shards(): tiles = lax.all_to_all(act, 'wide', split_axis=2, concat_axis=1, tiled=True)  20 us
    slice x9, local copies, waits for them, and re-layouts, spatial_forward(): padded[:, row_off:row_off + row_count, col_off:col_off + col_count, :]  16.8 us
    reduce_scatter x1, waiting for transfers between devices, shards(): lax.psum_scatter(partial_pair[1], 'dp', scatter_dimension=0, tiled=True)  15.9 us
    dot_general x9, matrix products, spatial_backward(): lax.dot_general(window, grad_flat, CONTRACT_ROWS, preferred_element_type=...  13.3 us
  transfers between devices with their start and end apart: 6, of which 5 were waited for; matrix products, arithmetic and copies ran while one was open for 22% of the time, Pallas kernels for 0%

commit v1 on v0

--- a/solution.py
+++ b/solution.py
@@ -2,6 +2,7 @@
 import jax.numpy as jnp
 from jax import lax
 from jax.sharding import PartitionSpec as P
+from jax.lax import axis_index, axis_size, ppermute
 
 G = 32
 FRAMES = 8
@@ -99,7 +100,15 @@
 def shards(clips, w_spatial, w_time, norm_gain, norm_bias, grad_out):
     group_count, frame_count, row_count, col_count, chan_count = clips.shape
     frames = clips.reshape(group_count * frame_count, row_count, col_count, chan_count)
-    weights = lax.all_gather(w_spatial, "dp", axis=1, tiled=True)
+    newest, carry_in, reached = (axis_size("dp"), axis_index("dp"), w_spatial.shape[1])
+    passed, local_out = (w_spatial, 1)
+    while local_out < newest:
+        gallery = []
+        for i0 in range(newest):
+            gallery.append((i0, (i0 - local_out) % newest))
+        passed = jnp.concatenate([passed, ppermute(passed, "dp", gallery)], 1)
+        local_out = 2 * local_out
+    weights = jnp.roll(passed, carry_in * reached, 1)
     hidden = spatial_forward(frames, weights).astype(jnp.bfloat16)
     preact, normed, inv_std = norm_forward(hidden, norm_gain, norm_bias)
     act = (

time: 339 us -> 368 us (1.086)
  local copies, waits for them, and re-layouts: 49.4 us -> 58.3 us
  waiting for transfers between devices: 196 us -> 204 us
  starting transfers between devices: 6.55 us -> 10.5 us
  matrix products: 36.5 us -> 40.3 us
    ppermute x0 -> x2, waiting for transfers between devices: none -> 44.4 us  [shards(): passed = jnp.concatenate([passed, ppermute(passed, 'dp', gallery)], 1)]
    all_gather x1 -> x0, waiting for transfers between devices: 32.4 us -> none  [shards(): weights = lax.all_gather(w_spatial, 'dp', axis=1, tiled=True)]
    dot_general x9, matrix products: 9.93 us -> 15.4 us  [spatial_backward(): lax.dot_general(flipped, tap_weight, CONTRACT_COLS, preferred_element_typ...]
    ppermute x0 -> x2, starting transfers between devices: none -> 5.42 us  [shards(): passed = jnp.concatenate([passed, ppermute(passed, 'dp', gallery)], 1)]
    reduce_scatter x1, waiting for transfers between devices: 15.9 us -> 10.7 us  [shards(): lax.psum_scatter(partial_pair[1], 'dp', scatter_dimension=0, tiled=True)]
    unnamed x47 -> x48, local copies, waits for them, and re-layouts: 27.9 us -> 32.5 us
    unnamed x7 -> x6, waiting for transfers between devices: 109 us -> 111 us
  transfers between devices with their start and end apart: 6 -> 7, of which waited for: 5 -> 6; matrix products, arithmetic and copies ran while one was open for 22% -> 24% of each run, Pallas kernels for 0% -> 0%
where the time goes in v1:
time: 368 us; the launch traced here: 366 us
  waiting for transfers between devices  204 us (55%)
  local copies, waits for them, and re-layouts  58.3 us (16%)
  matrix products  40.3 us (11%)
  blocking collectives  20.3 us (6%)
  other arithmetic  17.9 us (5%)
  between operations  14.2 us (4%)
  starting transfers between devices  10.5 us (3%)
    unnamed x6, waiting for transfers between devices  111 us
    ppermute x2, waiting for transfers between devices, shards(): passed = jnp.concatenate([passed, ppermute(passed, 'dp', gallery)], 1)  44.4 us
    reduce_scatter x1, waiting for transfers between devices, shards(): lax.psum_scatter(partial_pair[0], 'dp', scatter_dimension=0, tiled=True)  38.6 us
    unnamed x48, local copies, waits for them, and re-layouts  32.5 us
    all_to_all x1, blocking collectives, shards(): tiles = lax.all_to_all(act, 'wide', split_axis=2, concat_axis=1, tiled=True)  20.3 us
    slice x9, local copies, waits for them, and re-layouts, spatial_forward(): padded[:, row_off:row_off + row_count, col_off:col_off + col_count, :]  19.4 us
    dot_general x9, matrix products, spatial_backward(): lax.dot_general(flipped, tap_weight, CONTRACT_COLS, preferred_element_typ...  15.4 us
    dot_general x9, matrix products, spatial_backward(): lax.dot_general(window, grad_flat, CONTRACT_ROWS, preferred_element_type=...  13.3 us
  transfers between devices with their start and end apart: 7, of which 6 were waited for; matrix products, arithmetic and copies ran while one was open for 24% of the time, Pallas kernels for 0%

profile of v1, /device:TPU:0, one launch (start us, length us, event | category | flops | bytes accessed | tf_op | source)
XLA Modules:
  0.0 366.0 jit_solution(153292731527029675)
XLA Ops:
  7.2 4.0 %collective-permute-start = (bf16[4608,128]{1,0:T(8,128)(2,1)}, bf16[4608,128]{1,0:T(8,128)(2,1)S(1)}, u32[]{:S(2)}, u32[]{:S(2)}) collective-permute-start(bf16[4608,128]{1,0:T(8,128)(2,1)} %param.7), channel_id=1, source_target_pairs={{0,24},{8,0},{16,8},{24,16},{1,25},{9,1},{17,9},{25,17},{2,26},{10... | collective-permute-start | bytes 3538952 | tf_op jit(solution)/shard_map/ppermute | solution.py:109
  11.1 25.5 %collective-permute-done = bf16[4608,128]{1,0:T(8,128)(2,1)S(1)} collective-permute-done((bf16[4608,128]{1,0:T(8,128)(2,1)}, bf16[4608,128]{1,0:T(8,128)(2,1)S(1)}, u32[]{:S(2)}, u32[]{:S(2)}) %collective-permute-start) | collective-permute-done | bytes 1179680 | tf_op jit(solution)/shard_map/ppermute | solution.py:109
  36.7 2.9 pad_maximum_fusion.1
  41.1 1.6 convolution_bitcast_fusion.14
  42.6 1.6 convolution_bitcast_fusion.13
  44.3 2.6 fusion.29
  46.8 4.9 %all-to-all-start = ((bf16[1,8,64,512]{3,2,0,1:T(8,128)(2,1)}), bf16[1,8,64,512]{3,2,0,1:T(8,128)(2,1)S(1)}, u32[]{:S(2)}, u32[]{:S(2)}) async-start(bf16[1,8,64,512]{3,2,0,1:T(8,128)(2,1)} %fusion.29), calls=%async_computation | async-start | bytes 1048576 | tf_op jit(solution)/shard_map/all_to_all | solution.py:125
  53.1 2.9 pad_slice_fusion.7
  56.0 2.0 copy.46
  58.0 2.1 copy.45
  60.1 2.1 copy.44
  62.1 2.0 copy.43
  64.2 2.1 copy.42
  66.2 2.1 copy.41
  68.3 2.1 copy.40
  70.4 2.0 copy.39
  73.2 18.8 %collective-permute-done.1 = bf16[4608,256]{1,0:T(8,128)(2,1)} collective-permute-done((bf16[4608,256]{1,0:T(8,128)(2,1)}, bf16[4608,256]{1,0:T(8,128)(2,1)}, u32[]{:S(2)}, u32[]{:S(2)}) %collective-permute-start.1) | collective-permute-done | bytes 2359328 | tf_op jit(solution)/shard_map/ppermute | solution.py:109
  92.1 2.0 constant_dynamic-update-slice_fusion.3
  94.9 2.0 constant_dynamic-update-slice_fusion
  102.6 1.7 fusion.97
  105.7 1.8 copy.58
  108.0 5.7 %reduce.16 = bf16[512,512]{1,0:T(8,128)(2,1)} reduce(bf16[512,1,1,512]{3,2,1,0:T(2,128)(2,1)} %bitcast.222, bf16[]{:T(256)} %broadcast.544), dimensions={1,2}, to_apply=%bitcast.196.reduce_sub_computation | reduce | bytes 1048578
  113.8 2.2 reshape.596
  116.0 20.3 %all_to_all.21 = bf16[8,2,16384]{2,1,0:T(2,128)(2,1)} all-to-all(bf16[8,2,16384]{2,1,0:T(2,128)(2,1)} %reshape.596), channel_id=1, replica_groups=mesh['dp'=4,'wide'=8] {'wide'}, dimensions={0} | all-to-all | bytes 1048576 | tf_op jit(solution)/shard_map/all_to_all | solution.py:119
  136.3 3.5 reshape.597
  142.5 1.9 pad_maximum_fusion
  144.5 3.7 %copy.53 = f32[1536,512]{0,1:T(8,128)} copy(f32[1536,512]{1,0:T(8,128)} %pad_maximum_fusion) | data formatting | bytes 6291456
  148.2 1.5 multiply_convert_fusion.1
  149.7 1.5 fusion.8
  154.1 1.5 fusion.5
  158.6 1.6 fusion.2
  163.1 9.7 %copy.51 = f32[4608,512]{0,1:T(8,128)} copy(f32[4608,512]{1,0:T(8,128)} %fusion) | data formatting | bytes 18874368
  172.8 15.7 %reduce-scatter.15.cloned.1.call-done = f32[64,1536]{1,0:T(8,128)} async-done(((f32[512,1536]{1,0:T(8,128)}), f32[64,1536]{1,0:T(8,128)}) %reduce-scatter.15.cloned.1.call-update) | async-done | bytes 393232
  188.5 2.1 copy.54
  191.4 1.7 pad_slice_fusion.15
  193.1 1.5 fusion.72
  194.7 94.9 %reduce-scatter.13.cloned.1.call-done = f32[64,4608]{1,0:T(8,128)} async-done(((f32[512,4608]{1,0:T(8,128)}), f32[64,4608]{1,0:T(8,128)}) %reduce-scatter.13.cloned.1.call-update) | async-done | bytes 1179664
  289.6 2.9 copy.52
  292.5 1.7 fusion.56
  294.1 1.7 fusion.60
  295.8 1.7 fusion.64
  297.5 1.7 fusion.68
  299.2 1.5 fusion.75
  300.7 1.5 fusion.79
  302.2 1.5 fusion.83
  303.8 2.6 fusion.26
  306.4 10.7 %reduce-scatter.11.cloned.1.call-done = f32[384,64]{1,0:T(8,128)} async-done(((f32[1536,64]{1,0:T(8,128)}), f32[384,64]{1,0:T(8,128)}) %reduce-scatter.11.cloned.1.call-update) | async-done | bytes 98320 | tf_op jit(solution)/shard_map/reduce_scatter | solution.py:145
  318.8 38.6 %reduce-scatter.9.cloned.1.call-done = f32[1152,64]{1,0:T(8,128)} async-done(((f32[4608,64]{1,0:T(8,128)}), f32[1152,64]{1,0:T(8,128)}) %reduce-scatter.9.cloned.1.call-update) | async-done | bytes 294928 | tf_op jit(solution)/shard_map/reduce_scatter | solution.py:144
  (94 shorter events, 27.8 us)
Async XLA Ops:
  7.2 29.5 %collective-permute-start = (bf16[4608,128]{1,0:T(8,128)(2,1)}, bf16[4608,128]{1,0:T(8,128)(2,1)S(1)}, u32[]{:S(2)}, u32[]{:S(2)}) collective-permute-start(bf16[4608,128]{1,0:T(8,128)(2,1)} %param.7), channel_id=1, source_target_pairs={{0,24},{8,0},{16,8},{24,16},{1,25},{9,1},{17,9},{25,17},{2,26},{10... | collective-permute-start | bytes 3538952 | tf_op jit(solution)/shard_map/ppermute | solution.py:109
  39.6 52.4 %collective-permute-start.1 = (bf16[4608,256]{1,0:T(8,128)(2,1)}, bf16[4608,256]{1,0:T(8,128)(2,1)}, u32[]{:S(2)}, u32[]{:S(2)}) collective-permute-start(bf16[4608,256]{1,0:T(8,128)(2,1)} %pad_maximum_fusion.1), channel_id=1, source_target_pairs={{0,16},{8,24},{16,0},{24,8},{1,17},{9,25},{17,1},{25,9},{2,18},{10... | collective-permute-start | bytes 7077896 | tf_op jit(solution)/shard_map/ppermute | solution.py:109
  44.3 28.2 %copy-start.1 = (bf16[4608,128]{1,0:T(8,128)(2,1)S(1)}, bf16[4608,128]{1,0:T(8,128)(2,1)}, u32[]{:S(2)}) copy-start(bf16[4608,128]{1,0:T(8,128)(2,1)} %param.7) | copy-start | bytes 3538948
  46.8 55.7 %all-to-all-start = ((bf16[1,8,64,512]{3,2,0,1:T(8,128)(2,1)}), bf16[1,8,64,512]{3,2,0,1:T(8,128)(2,1)S(1)}, u32[]{:S(2)}, u32[]{:S(2)}) async-start(bf16[1,8,64,512]{3,2,0,1:T(8,128)(2,1)} %fusion.29), calls=%async_computation | async-start | bytes 1048576 | tf_op jit(solution)/shard_map/all_to_all | solution.py:125
  51.7 136.8 %reduce-scatter.15.cloned.1.call-start = ((), (), s32[]{:S(2)}) async-start(), calls=%async_computation.9 | async-start | bytes 3538944
  72.4 24.6 %copy-start.7 = (bf16[1,4,128,512]{3,2,1,0:T(8,128)(2,1)S(1)}, bf16[1,4,128,512]{3,2,1,0:T(8,128)(2,1)}, u32[]{:S(2)}) copy-start(bf16[1,4,128,512]{3,2,1,0:T(8,128)(2,1)} %copy.46) | copy-start | bytes 1572868
  72.8 24.7 %copy-start.8 = (bf16[1,4,128,512]{3,2,1,0:T(8,128)(2,1)S(1)}, bf16[1,4,128,512]{3,2,1,0:T(8,128)(2,1)}, u32[]{:S(2)}) copy-start(bf16[1,4,128,512]{3,2,1,0:T(8,128)(2,1)} %copy.45) | copy-start | bytes 1572868
  73.2 24.7 %copy-start.9 = (bf16[1,4,128,512]{3,2,1,0:T(8,128)(2,1)S(1)}, bf16[1,4,128,512]{3,2,1,0:T(8,128)(2,1)}, u32[]{:S(2)}) copy-start(bf16[1,4,128,512]{3,2,1,0:T(8,128)(2,1)} %copy.44) | copy-start | bytes 1572868
  73.2 25.2 %copy-start.10 = (bf16[1,4,128,512]{3,2,1,0:T(8,128)(2,1)S(1)}, bf16[1,4,128,512]{3,2,1,0:T(8,128)(2,1)}, u32[]{:S(2)}) copy-start(bf16[1,4,128,512]{3,2,1,0:T(8,128)(2,1)} %copy.43) | copy-start | bytes 1572868
  94.1 4.8 %copy-start.3 = (bf16[1,1,4,128,512]{4,3,2,1,0:T(8,128)(2,1)S(1)}, bf16[1,1,4,128,512]{4,3,2,1,0:T(8,128)(2,1)}, u32[]{:S(2)}) copy-start(bf16[1,1,4,128,512]{4,3,2,1,0:T(8,128)(2,1)} %param.6) | copy-start | bytes 1572868
  94.1 5.3 %copy-start.11 = (bf16[1,4,128,512]{3,2,1,0:T(8,128)(2,1)S(1)}, bf16[1,4,128,512]{3,2,1,0:T(8,128)(2,1)}, u32[]{:S(2)}) copy-start(bf16[1,4,128,512]{3,2,1,0:T(8,128)(2,1)} %copy.42) | copy-start | bytes 1572868
  94.5 5.3 %copy-start.12 = (bf16[1,4,128,512]{3,2,1,0:T(8,128)(2,1)S(1)}, bf16[1,4,128,512]{3,2,1,0:T(8,128)(2,1)}, u32[]{:S(2)}) copy-start(bf16[1,4,128,512]{3,2,1,0:T(8,128)(2,1)} %copy.41) | copy-start | bytes 1572868
  94.9 5.3 %copy-start.13 = (bf16[1,4,128,512]{3,2,1,0:T(8,128)(2,1)S(1)}, bf16[1,4,128,512]{3,2,1,0:T(8,128)(2,1)}, u32[]{:S(2)}) copy-start(bf16[1,4,128,512]{3,2,1,0:T(8,128)(2,1)} %copy.40) | copy-start | bytes 1572868
  97.0 4.6 %copy-start = (bf16[4608,1024]{1,0:T(8,128)(2,1)}, bf16[4608,1024]{1,0:T(8,128)(2,1)S(1)}, u32[]{:S(2)}) copy-start(bf16[4608,1024]{1,0:T(8,128)(2,1)S(1)} %constant_dynamic-update-slice_fusion) | copy-start | bytes 28311556
  97.0 3.7 %copy-start.5 = (bf16[1,4,128,512]{3,2,1,0:T(8,128)(2,1)S(1)}, bf16[1,4,128,512]{3,2,1,0:T(8,128)(2,1)}, u32[]{:S(2)}) copy-start(bf16[1,4,128,512]{3,2,1,0:T(8,128)(2,1)} %copy.39) | copy-start | bytes 1572868
  99.3 3.2 copy-start.14
  99.3 3.2 copy-start.15
  101.6 39.5 %copy-start.2 = (bf16[1,8,64,512]{3,2,1,0:T(8,128)(2,1)S(1)}, bf16[1,8,64,512]{3,2,1,0:T(8,128)(2,1)}, u32[]{:S(2)}) copy-start(bf16[1,8,64,512]{3,2,1,0:T(8,128)(2,1)} %param.11) | copy-start | bytes 1572868
  144.5 11.2 %copy-start.4 = (bf16[1,1,4,128,512]{4,3,2,1,0:T(8,128)(2,1)S(1)}, bf16[1,1,4,128,512]{4,3,2,1,0:T(8,128)(2,1)}, u32[]{:S(2)}) copy-start(bf16[1,1,4,128,512]{4,3,2,1,0:T(8,128)(2,1)} %param.6) | copy-start | bytes 1572868
  148.2 141.4 %reduce-scatter.13.cloned.1.call-start = ((), (), s32[]{:S(2)}) async-start(), calls=%async_computation.8 | async-start | bytes 10616832
  172.8 144.4 %reduce-scatter.11.cloned.1.call-start = ((), (), s32[]{:S(2)}) async-start(), calls=%async_computation.7 | async-start | bytes 983040 | tf_op jit(solution)/shard_map/reduce_scatter | solution.py:145
  190.7 166.7 %reduce-scatter.9.cloned.1.call-start = ((), (), s32[]{:S(2)}) async-start(), calls=%async_computation.6 | async-start | bytes 2949120 | tf_op jit(solution)/shard_map/reduce_scatter | solution.py:144
  194.6 104.5 %copy-start.6 = (bf16[1,4,128,512]{3,2,1,0:T(8,128)(2,1)S(1)}, bf16[1,4,128,512]{3,2,1,0:T(8,128)(2,1)}, u32[]{:S(2)}) copy-start(bf16[1,4,128,512]{3,2,1,0:T(8,128)(2,1)} %get-tuple-element.23) | copy-start | bytes 1572868
Sparse Core Ops, SparseCore 0:
  148.3 40.1 reduce-scatter.14
  190.8 98.6 reduce-scatter.12
  292.5 24.6 reduce-scatter.10
  320.0 37.3 reduce-scatter.8
